TPU v7x, 512 devices: a whole 4x4x16 slice. The times are simulated.
512 devices in a mesh: fsdp: 64 (over x, z), tensor: 8 (over y, core).
Axes of the slice: x: 4, y: 4, z: 16, core: 2. Of those that a mesh axis runs over, the one named last changes fastest.
Arguments:
- gate_pre: bfloat16 [12288, 14336], P(('fsdp', 'tensor')), may hold values from -6 to 6
- up_pre: bfloat16 [12288, 14336], P(('fsdp', 'tensor')), may hold values from -6 to 6
- cotangent: bfloat16 [12288, 4096], P('fsdp'), may hold values from -6 to 6
- w_slots: bfloat16 [8, 192, 128, 128], P('tensor', 'fsdp'), may hold values from -0.15625 to 0.15625
- slot_ids: int32 [8, 192], P('tensor'), may hold values from -1 to 447, as said below
Outputs:
- d_gate: bfloat16 [12288, 14336], P(('fsdp', 'tensor'))
- d_up: bfloat16 [12288, 14336], P(('fsdp', 'tensor'))
- w_grad: float32 [8, 192, 128, 128], P('tensor', 'fsdp')
Inputs may be any that keep to these rules, and one draw needn't show every extreme that they name: `slot_ids`: in row t, slots s * 3 to s * 3 + 2 list the kept blocks owned by fsdp index s in tensor slice t as local row block * 32 + column block, filling the first slots and -1 in the rest; every owner has 2 or 3 kept blocks, some owner of every row exactly 3 and some exactly 2; no block id appears twice in a row.
All inputs are finite; a program needn't handle non-finite values.
Results may differ from a plain program's by a relative error of at most 0.0085.
Values may be sent and summed in bfloat16 or wider, within the bound.
No kernel may reach another device: no remote copies, remote signals or barrier semaphores. Data moves between devices by JAX's collectives and lax.ppermute only.
A program may use at most 128 MiB of HBM per device.

v0:
```python
import math
import jax
import jax.numpy as jnp
from jax import lax
from jax.sharding import PartitionSpec as P


def swiglu_value(gate_part, up_part):
    gate_f = gate_part.astype(jnp.float32)
    gate_sig = jax.nn.sigmoid(gate_f)
    return (gate_f * gate_sig * up_part.astype(jnp.float32)).astype(jnp.bfloat16)


def swiglu_grads(dh_part, gate_part, up_part):
    gate_f = gate_part.astype(jnp.float32)
    up_f = up_part.astype(jnp.float32)
    gate_sig = jax.nn.sigmoid(gate_f)
    dh_f = dh_part.astype(jnp.float32)
    grad_gate = (dh_f * up_f * (gate_sig * (1.0 + gate_f * (1.0 - gate_sig)))).astype(jnp.bfloat16)
    grad_up = (dh_f * (gate_f * gate_sig)).astype(jnp.bfloat16)
    return (grad_gate, grad_up)


def body(gate_pre, up_pre, cotangent, w_slots, slot_ids):
    n_fsdp = lax.axis_size("fsdp")
    block_size = w_slots.shape[2]
    token_count = cotangent.shape[0]
    model_width = cotangent.shape[1]
    col_count = model_width // block_size
    ff_dev = gate_pre.shape[1] // lax.axis_size("tensor")
    row_count = ff_dev // block_size
    slot_total = slot_ids.shape[1]
    cap_local = w_slots.shape[1]
    slot_list = slot_ids[0]
    usable = slot_list >= 0
    safe_ids = jnp.maximum(slot_list, 0)
    row_index = jnp.where(usable, safe_ids // col_count, row_count)
    col_index = safe_ids % col_count
    row_clip = jnp.minimum(row_index, row_count - 1)
    usable_f = usable.astype(jnp.float32)
    row_range = jnp.arange(row_count, dtype=jnp.int32)
    dy_blocks = cotangent.reshape(token_count, col_count, block_size)
    gate_t, up_t = (
        lax.all_to_all(gate_pre, "tensor", split_axis=1, concat_axis=0, tiled=True),
        lax.all_to_all(up_pre, "tensor", split_axis=1, concat_axis=0, tiled=True),
    )
    hidden = swiglu_value(gate_t, up_t)
    start_sum = jnp.zeros((token_count, row_count, block_size), jnp.float32)
    running = start_sum
    shard_piece = lax.all_gather(w_slots, "fsdp", axis=1, tiled=True)
    slot_count = shard_piece.shape[1]
    sub_size = math.gcd(slot_count, 48)
    rows_part = row_index.reshape(slot_count // sub_size, sub_size)
    cols_part = col_index.reshape(slot_count // sub_size, sub_size)
    weight_part = shard_piece[0].reshape(slot_count // sub_size, sub_size, block_size, block_size)

    def advance(carried, packed_item):
        rows_now, cols_now, weight_now = packed_item
        dy_picked = jnp.take(dy_blocks, cols_now, axis=1)
        contrib = jnp.einsum(
            "tsb,sab->tsa", dy_picked, weight_now, preferred_element_type=jnp.float32
        )
        onehot = (rows_now[:, None] == row_range[None, :]).astype(jnp.float32)
        added = jnp.einsum("tsa,sr->tra", contrib, onehot, precision=lax.Precision.HIGHEST)
        return (carried + added, None)

    running, _ = lax.scan(advance, running, (rows_part, cols_part, weight_part))
    d_hidden = running.reshape(token_count, ff_dev).astype(jnp.bfloat16)
    grad_scale = 1.0 / math.sqrt(token_count * n_fsdp)
    hidden_blocks = hidden.reshape(token_count, row_count, block_size)
    group_size = math.gcd(slot_total, 48)
    group_count = slot_total // group_size

    def partial_group(packed_item):
        rows_now, cols_now, scale_now = packed_item
        h_picked = jnp.take(hidden_blocks, rows_now, axis=1)
        dy_picked = jnp.take(dy_blocks, cols_now, axis=1)
        product = jnp.einsum(
            "tsa,tsb->sab", h_picked, dy_picked, preferred_element_type=jnp.float32
        )
        return (product * scale_now[:, None, None]).astype(jnp.bfloat16)

    partials = lax.map(
        partial_group,
        (
            row_clip.reshape(group_count, group_size),
            col_index.reshape(group_count, group_size),
            (grad_scale * usable_f).reshape(group_count, group_size),
        ),
    )
    partials = partials.reshape(slot_total, block_size, block_size)
    arrived = lax.all_to_all(partials, "fsdp", split_axis=0, concat_axis=0, tiled=True)
    w_grad = (
        arrived.astype(jnp.float32)
        .reshape(n_fsdp, cap_local, block_size, block_size)
        .sum(axis=0)[None]
    )
    grad_gate_t, grad_up_t = swiglu_grads(d_hidden, gate_t, up_t)
    d_gate, d_up = (
        lax.all_to_all(grad_gate_t, "tensor", split_axis=0, concat_axis=1, tiled=True),
        lax.all_to_all(grad_up_t, "tensor", split_axis=0, concat_axis=1, tiled=True),
    )
    return (d_gate, d_up, w_grad)


def solution(mesh):
    placed = (
        P(("fsdp", "tensor"), None),
        P(("fsdp", "tensor"), None),
        P("fsdp", None),
        P("tensor", "fsdp", None, None),
        P("tensor", None),
    )
    return jax.shard_map(
        body,
        mesh=mesh,
        in_specs=placed,
        out_specs=(
            P(("fsdp", "tensor"), None),
            P(("fsdp", "tensor"), None),
            P("tensor", "fsdp", None, None),
        ),
        check_vma=False,
    )
```

profile of v0, /device:TPU:8, one launch (start us, length us, event | category | flops | bytes accessed | tf_op | source)
XLA Modules:
  0.0 586.6 jit_solution(15510980413584426776)
XLA Ops:
  7.2 0.0 copy-start
  7.2 0.0 all-gather.2.cloned.1.call-start
  7.2 0.7 all-gather.2.cloned.1.call-update
  7.9 2.0 copy.45
  9.9 9.9 %all-to-all-start = ((bf16[24,8,1792]{2,0,1:T(8,128)(2,1)}), bf16[24,8,1792]{2,0,1:T(8,128)(2,1)}, u32[]{:S(2)}, u32[]{:S(2)}) async-start(bf16[24,8,1792]{2,0,1:T(8,128)(2,1)} %bitcast.85), calls=%async_computation | async-start | bytes 1376256 | tf_op jit(solution)/shard_map/all_to_all | solution.py:45
  19.8 0.0 copy-done.4
  19.8 0.1 ne.31
  19.9 0.1 ge.24
  20.0 0.1 rem.19
  20.1 0.1 div.21
  20.2 0.9 copy.44
  21.1 0.4 copy_bitcast_fusion
  21.6 9.0 %all-to-all-done = bf16[24,8,1792]{2,0,1:T(8,128)(2,1)} async-done(((bf16[24,8,1792]{2,0,1:T(8,128)(2,1)}), bf16[24,8,1792]{2,0,1:T(8,128)(2,1)}, u32[]{:S(2)}, u32[]{:S(2)}) %all-to-all-start) | async-done | bytes 688160 | tf_op jit(solution)/shard_map/all_to_all | solution.py:45
  30.6 5.5 all-to-all-start.1
  36.1 2.3 convert_bitcast_fusion.1
  38.4 127.6 %all-gather.2.cloned.1.call-done = bf16[1,192,128,128]{3,2,0,1:T(8,128)(2,1)} async-done(((bf16[1,3,128,128]{3,2,0,1:T(8,128)(2,1)}), bf16[1,192,128,128]{3,2,0,1:T(8,128)(2,1)}) %all-gather.2.cloned.1.call-update) | async-done | bytes 6291472 | tf_op jit(solution)/shard_map/all_gather | solution.py:50
  166.0 46.6 %while.22 = (s32[]{:T(128)}, f32[192,14,128]{2,1,0:T(8,128)}, s32[4,48]{1,0:T(4,128)S(1)}, bf16[4,48,128,128]{3,2,1,0:T(8,128)(2,1)}, s32[4,48]{1,0:T(4,128)S(1)...) while((s32[]{:T(128)}, f32[192,14,128]{2,1,0:T(8,128)}, s32[4,48]{1,0:T(4,128)S(1)}, ...), condition=%wide.region_1.3_spmd.clone, body=%wide.region_0.2_spmd.clone.sunk | while | flops 502040512 | bytes 31856200 | solution.py:67
  166.1 2.3 gather_fusion.2
  168.4 3.4 fusion.64
  171.8 4.7 bitcast_add_fusion.2
  176.5 1.2 copy-done.2
  177.7 2.3 gather_fusion.2
  180.0 3.4 fusion.64
  183.5 4.7 bitcast_add_fusion.2
  188.2 1.2 copy-done.2
  189.4 2.3 gather_fusion.2
  191.7 3.4 fusion.64
  195.1 4.7 bitcast_add_fusion.2
  199.8 1.2 copy-done.2
  201.0 2.3 gather_fusion.2
  203.3 3.4 fusion.64
  206.8 4.7 bitcast_add_fusion.2
  211.5 1.2 copy-done.2
  212.6 2.7 convert_convert_fusion
  215.3 2.6 reshape.111
  217.9 0.0 all-to-all-done.1
  217.9 3.5 multiply_convert_fusion.2
  221.4 5.0 all-to-all-start.3
  226.4 2.3 convert_bitcast_fusion
  228.7 2.6 reshape.113
  231.3 2.7 reshape.112
  234.0 2.3 multiply_convert_fusion.1
  236.3 1.0 copy.30
  237.3 0.0 all-to-all-done.3
  237.3 5.4 all-to-all-start.2
  242.7 43.6 %while.21 = (s32[]{:T(128)}, bf16[4,48,128,128]{3,2,1,0:T(8,128)(2,1)}, s32[4,48]{1,0:T(4,128)S(1)}, bf16[192,14,128]{2,0,1:T(8,128)(2,1)}, s32[4,48]{1,0:T(4,12...) while((s32[]{:T(128)}, bf16[4,48,128,128]{3,2,1,0:T(8,128)(2,1)}, ...), condition=%wide.region_3.5_spmd, body=%wide.region_2.4_spmd.sunk | while | flops 305924832 | bytes 15739437 | solution.py:83
  242.8 3.5 gather_fusion.1
  246.3 2.4 gather_fusion
  248.7 4.9 bitcast_dynamic-update-slice_fusion.2
  253.7 3.5 gather_fusion.1
  257.2 2.4 gather_fusion
  259.6 4.9 bitcast_dynamic-update-slice_fusion.2
  264.5 3.5 gather_fusion.1
  268.0 2.4 gather_fusion
  270.4 4.9 bitcast_dynamic-update-slice_fusion.2
  275.4 3.5 gather_fusion.1
  278.9 2.4 gather_fusion
  281.3 4.9 bitcast_dynamic-update-slice_fusion.2
  286.3 0.0 all-to-all-done.2
  286.3 9.7 %all-to-all-start.4 = ((bf16[192,128,128]{2,1,0:T(8,128)(2,1)}), bf16[192,128,128]{2,1,0:T(8,128)(2,1)}, u32[]{:S(2)}, u32[]{:S(2)}) async-start(bf16[192,128,128]{2,1,0:T(8,128)(2,1)} %bitcast.111), calls=%async_computation.4 | async-start | bytes 12582912 | tf_op jit(solution)/shard_map/all_to_all | solution.py:92
  295.9 2.0 copy.36
  297.9 2.0 copy.35
  299.9 275.3 %all-to-all-done.4 = bf16[192,128,128]{2,1,0:T(8,128)(2,1)} async-done(((bf16[192,128,128]{2,1,0:T(8,128)(2,1)}), bf16[192,128,128]{2,1,0:T(8,128)(2,1)}, u32[]{:S(2)}, u32[]{:S(2)}) %all-to-all-start.4) | async-done | bytes 6291488 | tf_op jit(solution)/shard_map/all_to_all | solution.py:92
  575.2 4.6 convert_reduce_fusion
  (54 shorter events, 0.3 us)
Async XLA Ops:
  7.2 14.0 %copy-start = (bf16[192,4096]{1,0:T(8,128)(2,1)S(1)}, bf16[192,4096]{1,0:T(8,128)(2,1)}, u32[]{:S(2)}) copy-start(bf16[192,4096]{1,0:T(8,128)(2,1)} %param.13) | copy-start | bytes 4718596
  7.2 12.6 %copy-start.4 = (s32[1,192]{1,0:T(1,128)S(1)}, s32[1,192]{1,0:T(1,128)}, u32[]{:S(2)}) copy-start(s32[1,192]{1,0:T(1,128)} %param.15) | copy-start | bytes 2308
  7.2 13.0 %copy-start.3 = (bf16[24,14336]{1,0:T(8,128)(2,1)S(1)}, bf16[24,14336]{1,0:T(8,128)(2,1)}, u32[]{:S(2)}) copy-start(bf16[24,14336]{1,0:T(8,128)(2,1)} %param.11) | copy-start | bytes 2064388
  7.2 158.8 %all-gather.2.cloned.1.call-start = ((), (), s32[]{:S(2)}) async-start(), calls=%async_computation.5 | async-start | bytes 6389760 | tf_op jit(solution)/shard_map/all_gather | solution.py:50
  9.9 20.6 %all-to-all-start = ((bf16[24,8,1792]{2,0,1:T(8,128)(2,1)}), bf16[24,8,1792]{2,0,1:T(8,128)(2,1)}, u32[]{:S(2)}, u32[]{:S(2)}) async-start(bf16[24,8,1792]{2,0,1:T(8,128)(2,1)} %bitcast.85), calls=%async_computation | async-start | bytes 1376256 | tf_op jit(solution)/shard_map/all_to_all | solution.py:45
  30.6 187.4 %all-to-all-start.1 = ((bf16[24,8,1792]{2,0,1:T(8,128)(2,1)}), bf16[24,8,1792]{2,0,1:T(8,128)(2,1)}, u32[]{:S(2)}, u32[]{:S(2)}) async-start(bf16[24,8,1792]{2,0,1:T(8,128)(2,1)} %bitcast.112), calls=%async_computation.1 | async-start | bytes 1376256 | tf_op jit(solution)/shard_map/all_to_all | solution.py:44
  168.4 3.4 copy-start.1
  176.5 1.2 copy-start.2
  180.0 3.4 copy-start.1
  188.2 1.2 copy-start.2
  191.7 3.4 copy-start.1
  199.8 1.2 copy-start.2
  203.3 3.4 copy-start.1
  211.5 1.2 copy-start.2
  221.4 15.9 %all-to-all-start.3 = ((bf16[8,24,1792]{2,1,0:T(8,128)(2,1)}), bf16[8,24,1792]{2,1,0:T(8,128)(2,1)}, u32[]{:S(2)}, u32[]{:S(2)}) async-start(bf16[8,24,1792]{2,1,0:T(8,128)(2,1)} %get-tuple-element.173), calls=%async_computation.3 | async-start | bytes 1376256 | tf_op jit(solution)/shard_map/all_to_all | solution.py:101
  237.3 48.9 %all-to-all-start.2 = ((bf16[8,24,1792]{2,1,0:T(8,128)(2,1)}), bf16[8,24,1792]{2,1,0:T(8,128)(2,1)}, u32[]{:S(2)}, u32[]{:S(2)}) async-start(bf16[8,24,1792]{2,1,0:T(8,128)(2,1)} %get-tuple-element.174), calls=%async_computation.2 | async-start | bytes 1376256 | tf_op jit(solution)/shard_map/all_to_all | solution.py:100
  286.3 288.9 %all-to-all-start.4 = ((bf16[192,128,128]{2,1,0:T(8,128)(2,1)}), bf16[192,128,128]{2,1,0:T(8,128)(2,1)}, u32[]{:S(2)}, u32[]{:S(2)}) async-start(bf16[192,128,128]{2,1,0:T(8,128)(2,1)} %bitcast.111), calls=%async_computation.4 | async-start | bytes 12582912 | tf_op jit(solution)/shard_map/all_to_all | solution.py:92
Sparse Core Ops, SparseCore 0:
  11.0 155.0 all-gather.1
where the time goes:
time: 588 us; the launch traced here: 587 us
  waiting for transfers between devices  413 us (70%)
  local copies, waits for them, and re-layouts  54.2 us (9%)
  matrix products  52.1 us (9%)
  starting transfers between devices  35.5 us (6%)
  other arithmetic  17.8 us (3%)
  between operations  14.1 us (2%)
    all_to_all x1, waiting for transfers between devices, body(): lax.all_to_all(partials, 'fsdp', split_axis=0, concat_axis=0, tiled=True)  275 us
    all_gather x1, waiting for transfers between devices, body(): shard_piece = lax.all_gather(w_slots, 'fsdp', axis=1, tiled=True)  128 us
    dot_general x4, matrix products, partial_group(): jnp.einsum('tsa,tsb->sab', h_picked, dy_picked, preferred_element_type=jn...  19.7 us
    dot_general x4, matrix products, advance(): jnp.einsum('tsa,sr->tra', contrib, onehot, precision=lax.Precision.HIGHEST)  18.7 us
    gather x4, local copies, waits for them, and re-layouts, partial_group(): h_picked = jnp.take(hidden_blocks, rows_now, axis=1)  14 us
    dot_general x4, matrix products, advance(): jnp.einsum('tsb,sab->tsa', dy_picked, weight_now, preferred_element_type=...  13.7 us
  transfers between devices with their start and end apart: 6, of which 3 were waited for; matrix products, arithmetic and copies ran while one was open for 19% of the time, Pallas kernels for 0%

commit v1 on v0

--- a/solution.py
+++ b/solution.py
@@ -47,7 +47,9 @@
     hidden = swiglu_value(gate_t, up_t)
     start_sum = jnp.zeros((token_count, row_count, block_size), jnp.float32)
     running = start_sum
-    shard_piece = lax.all_gather(w_slots, "fsdp", axis=1, tiled=True)
+    shard_piece = jnp.concatenate(
+        lax.all_to_all(jnp.stack([w_slots] * lax.axis_size("fsdp")), "fsdp", 0, 0), axis=1
+    )
     slot_count = shard_piece.shape[1]
     sub_size = math.gcd(slot_count, 48)
     rows_part = row_index.reshape(slot_count // sub_size, sub_size)

time: 588 us -> 737 us (1.25)
  waiting for transfers between devices: 413 us -> 550 us
  blocking collectives: 0 us -> 19.6 us
  between operations: 14.1 us -> 0.74 us
    all_to_all x1, waiting for transfers between devices: 9 us -> 275 us  [body(): lax.all_to_all(jnp.stack([w_slots] * lax.axis_size('fsdp')), 'fsdp', 0, 0)]
    all_gather x1 -> x0, waiting for transfers between devices: 128 us -> none  [body(): shard_piece = lax.all_gather(w_slots, 'fsdp', axis=1, tiled=True)]
    all_to_all x0 -> x1, blocking collectives: none -> 19.6 us  [body(): lax.all_to_all(up_pre, 'tensor', split_axis=1, concat_axis=0, tiled=True)]
  transfers between devices with their start and end apart: 6 -> 5, of which waited for: 3 -> 2; matrix products, arithmetic and copies ran while one was open for 19% -> 15% of each run, Pallas kernels for 0% -> 0%
where the time goes in v1:
time: 737 us; the launch traced here: 736 us
  waiting for transfers between devices  550 us (75%)
  local copies, waits for them, and re-layouts  58.4 us (8%)
  matrix products  52.1 us (7%)
  starting transfers between devices  37.5 us (5%)
  blocking collectives  19.6 us (3%)
  other arithmetic  16.7 us (2%)
    all_to_all x1, waiting for transfers between devices, body(): lax.all_to_all(partials, 'fsdp', split_axis=0, concat_axis=0, tiled=True)  275 us
    all_to_all x1, waiting for transfers between devices, body(): lax.all_to_all(jnp.stack([w_slots] * lax.axis_size('fsdp')), 'fsdp', 0, 0)  275 us
    dot_general x4, matrix products, partial_group(): jnp.einsum('tsa,tsb->sab', h_picked, dy_picked, preferred_element_type=jn...  19.7 us
    all_to_all x1, blocking collectives, body(): lax.all_to_all(up_pre, 'tensor', split_axis=1, concat_axis=0, tiled=True)  19.6 us
    dot_general x4, matrix products, advance(): jnp.einsum('tsa,sr->tra', contrib, onehot, precision=lax.Precision.HIGHEST)  18.7 us
    all_to_all x1, starting transfers between devices, body(): lax.all_to_all(jnp.stack([w_slots] * lax.axis_size('fsdp')), 'fsdp', 0, 0)  14.8 us
  transfers between devices with their start and end apart: 5, of which 2 were waited for; matrix products, arithmetic and copies ran while one was open for 15% of the time, Pallas kernels for 0%

profile of v1, /device:TPU:8, one launch (start us, length us, event | category | flops | bytes accessed | tf_op | source)
XLA Modules:
  0.0 735.6 jit_solution(16821463487552826676)
XLA Ops:
  0.6 0.0 copy-start
  0.7 1.3 copy.44
  1.9 19.6 %all_to_all.68 = bf16[24,8,1792]{2,0,1:T(8,128)(2,1)} all-to-all(bf16[24,8,1792]{2,0,1:T(8,128)(2,1)S(1)} %bitcast.112), channel_id=1, replica_groups=mesh['fsdp'=64,'tensor'=8] {'tensor'}, dimensions={1} | all-to-all | bytes 1376256 | tf_op jit(solution)/shard_map/all_to_all | solution.py:45
  21.5 0.0 copy-done.5
  21.5 4.2 stack.2
  25.7 14.8 %all-to-all-start = ((bf16[64,1,3,128,128]{4,3,2,1,0:T(8,128)(2,1)}), bf16[64,1,3,128,128]{4,3,2,1,0:T(8,128)(2,1)}, u32[]{:S(2)}, u32[]{:S(2)}) async-start(bf16[64,1,3,128,128]{4,3,2,1,0:T(8,128)(2,1)} %stack.2), calls=%async_computation | async-start | bytes 12582912 | tf_op jit(solution)/shard_map/all_to_all | solution.py:51
  40.6 0.1 ne.31
  40.7 0.1 ge.24
  40.8 0.1 rem.19
  40.9 0.1 div.21
  41.0 0.9 copy.43
  41.9 0.4 copy_bitcast_fusion
  42.3 0.7 copy-done.3
  43.0 1.2 convert_bitcast_fusion.1
  44.2 274.9 %all-to-all-done = bf16[64,1,3,128,128]{4,3,2,1,0:T(8,128)(2,1)} async-done(((bf16[64,1,3,128,128]{4,3,2,1,0:T(8,128)(2,1)}), bf16[64,1,3,128,128]{4,3,2,1,0:T(8,128)(2,1)}, u32[]{:S(2)}, u32[]{:S(2)}) %all-to-all-start) | async-done | bytes 6291488 | tf_op jit(solution)/shard_map/all_to_all | solution.py:51
  319.1 5.6 all-to-all-start.2
  324.7 46.6 %while.22 = (s32[]{:T(128)}, f32[192,14,128]{2,1,0:T(8,128)}, s32[4,48]{1,0:T(4,128)S(1)}, bf16[4,48,128,128]{3,2,1,0:T(8,128)(2,1)}, s32[4,48]{1,0:T(4,128)S(1)...) while((s32[]{:T(128)}, f32[192,14,128]{2,1,0:T(8,128)}, s32[4,48]{1,0:T(4,128)S(1)}, ...), condition=%wide.region_1.3_spmd.clone, body=%wide.region_0.2_spmd.clone.sunk | while | flops 502040512 | bytes 31856200 | solution.py:69
  324.7 2.3 gather_fusion.2
  327.0 3.4 fusion.64
  330.5 4.7 bitcast_add_fusion.2
  335.1 1.2 copy-done.2
  336.4 2.3 gather_fusion.2
  338.7 3.4 fusion.64
  342.1 4.7 bitcast_add_fusion.2
  346.8 1.2 copy-done.2
  348.0 2.3 gather_fusion.2
  350.3 3.4 fusion.64
  353.8 4.7 bitcast_add_fusion.2
  358.5 1.2 copy-done.2
  359.7 2.3 gather_fusion.2
  362.0 3.4 fusion.64
  365.4 4.7 bitcast_add_fusion.2
  370.1 1.2 copy-done.2
  371.3 2.7 convert_convert_fusion
  374.0 2.6 reshape.114
  376.6 0.0 all-to-all-done.2
  376.6 3.5 multiply_convert_fusion.2
  380.1 4.8 all-to-all-start.4
  384.9 2.3 convert_bitcast_fusion
  387.2 2.6 reshape.116
  389.8 2.7 reshape.115
  392.4 2.3 multiply_convert_fusion.1
  394.7 1.0 copy.29
  395.8 0.0 all-to-all-done.4
  395.8 5.6 all-to-all-start.3
  401.3 43.6 %while.21 = (s32[]{:T(128)}, bf16[4,48,128,128]{3,2,1,0:T(8,128)(2,1)}, s32[4,48]{1,0:T(4,128)S(1)}, bf16[192,14,128]{2,0,1:T(8,128)(2,1)}, s32[4,48]{1,0:T(4,12...) while((s32[]{:T(128)}, bf16[4,48,128,128]{3,2,1,0:T(8,128)(2,1)}, ...), condition=%wide.region_3.5_spmd, body=%wide.region_2.4_spmd.sunk | while | flops 305924832 | bytes 15739437 | solution.py:85
  401.4 3.5 gather_fusion.1
  404.9 2.4 gather_fusion
  407.3 4.9 bitcast_dynamic-update-slice_fusion.2
  412.3 3.5 gather_fusion.1
  415.8 2.4 gather_fusion
  418.2 4.9 bitcast_dynamic-update-slice_fusion.2
  423.2 3.5 gather_fusion.1
  426.7 2.4 gather_fusion
  429.1 4.9 bitcast_dynamic-update-slice_fusion.2
  434.1 3.5 gather_fusion.1
  437.6 2.4 gather_fusion
  440.0 4.9 bitcast_dynamic-update-slice_fusion.2
  445.0 0.0 all-to-all-done.3
  445.0 6.7 all-to-all-start.5
  451.7 2.0 copy.35
  453.7 2.0 copy.34
  455.7 275.3 %all-to-all-done.5 = bf16[192,128,128]{2,1,0:T(8,128)(2,1)} async-done(((bf16[192,128,128]{2,1,0:T(8,128)(2,1)}), bf16[192,128,128]{2,1,0:T(8,128)(2,1)}, u32[]{:S(2)}, u32[]{:S(2)}) %all-to-all-start.5) | async-done | bytes 6291488 | tf_op jit(solution)/shard_map/all_to_all | solution.py:94
  731.0 4.6 convert_reduce_fusion
  (57 shorter events, 0.4 us)
Async XLA Ops:
  0.6 41.2 %copy-start = (bf16[192,4096]{1,0:T(8,128)(2,1)S(1)}, bf16[192,4096]{1,0:T(8,128)(2,1)}, u32[]{:S(2)}) copy-start(bf16[192,4096]{1,0:T(8,128)(2,1)} %param.13) | copy-start | bytes 4718596
  0.6 20.9 %copy-start.5 = (bf16[1,3,128,128]{3,2,1,0:T(8,128)(2,1)S(1)}, bf16[1,3,128,128]{3,2,1,0:T(8,128)(2,1)}, u32[]{:S(2)}) copy-start(bf16[1,3,128,128]{3,2,1,0:T(8,128)(2,1)} %param.14) | copy-start | bytes 294916
  25.7 14.9 %copy-start.6 = (s32[1,192]{1,0:T(1,128)S(1)}, s32[1,192]{1,0:T(1,128)}, u32[]{:S(2)}) copy-start(s32[1,192]{1,0:T(1,128)} %param.15) | copy-start | bytes 2308
  25.7 15.3 %copy-start.4 = (bf16[24,14336]{1,0:T(8,128)(2,1)S(1)}, bf16[24,14336]{1,0:T(8,128)(2,1)}, u32[]{:S(2)}) copy-start(bf16[24,14336]{1,0:T(8,128)(2,1)} %param.11) | copy-start | bytes 2064388
  25.7 293.4 %all-to-all-start = ((bf16[64,1,3,128,128]{4,3,2,1,0:T(8,128)(2,1)}), bf16[64,1,3,128,128]{4,3,2,1,0:T(8,128)(2,1)}, u32[]{:S(2)}, u32[]{:S(2)}) async-start(bf16[64,1,3,128,128]{4,3,2,1,0:T(8,128)(2,1)} %stack.2), calls=%async_computation | async-start | bytes 12582912 | tf_op jit(solution)/shard_map/all_to_all | solution.py:51
  41.9 1.1 copy-start.3
  319.1 57.5 %all-to-all-start.2 = ((bf16[24,8,1792]{2,0,1:T(8,128)(2,1)}), bf16[24,8,1792]{2,0,1:T(8,128)(2,1)}, u32[]{:S(2)}, u32[]{:S(2)}) async-start(bf16[24,8,1792]{2,0,1:T(8,128)(2,1)} %bitcast.111), calls=%async_computation.2 | async-start | bytes 1376256 | tf_op jit(solution)/shard_map/all_to_all | solution.py:44
  327.0 3.4 copy-start.1
  335.1 1.2 copy-start.2
  338.7 3.4 copy-start.1
  346.8 1.2 copy-start.2
  350.3 3.4 copy-start.1
  358.5 1.2 copy-start.2
  362.0 3.4 copy-start.1
  370.1 1.2 copy-start.2
  380.1 15.7 %all-to-all-start.4 = ((bf16[8,24,1792]{2,1,0:T(8,128)(2,1)}), bf16[8,24,1792]{2,1,0:T(8,128)(2,1)}, u32[]{:S(2)}, u32[]{:S(2)}) async-start(bf16[8,24,1792]{2,1,0:T(8,128)(2,1)} %get-tuple-element.173), calls=%async_computation.4 | async-start | bytes 1376256 | tf_op jit(solution)/shard_map/all_to_all | solution.py:103
  395.8 49.2 %all-to-all-start.3 = ((bf16[8,24,1792]{2,1,0:T(8,128)(2,1)}), bf16[8,24,1792]{2,1,0:T(8,128)(2,1)}, u32[]{:S(2)}, u32[]{:S(2)}) async-start(bf16[8,24,1792]{2,1,0:T(8,128)(2,1)} %get-tuple-element.174), calls=%async_computation.3 | async-start | bytes 1376256 | tf_op jit(solution)/shard_map/all_to_all | solution.py:102
  445.0 286.0 %all-to-all-start.5 = ((bf16[192,128,128]{2,1,0:T(8,128)(2,1)}), bf16[192,128,128]{2,1,0:T(8,128)(2,1)}, u32[]{:S(2)}, u32[]{:S(2)}) async-start(bf16[192,128,128]{2,1,0:T(8,128)(2,1)} %bitcast.110), calls=%async_computation.5 | async-start | bytes 12582912 | tf_op jit(solution)/shard_map/all_to_all | solution.py:94
